TPU v7x, 32 devices: a whole 2x2x4 slice. The times are simulated.
32 devices in a mesh: dp: 4 (over z), expert: 4 (over y, core), loop: 2 (over x).
Axes of the slice: x: 2, y: 2, z: 4, core: 2. Of those that a mesh axis runs over, the one named last changes fastest.
Arguments:
- x_send: bfloat16 [512, 4096], P(('dp', 'expert', 'loop')), may hold values from -6 to 6
- cot_send: bfloat16 [512, 4096], P(('dp', 'expert', 'loop')), may hold values from -6 to 6
- counts: int32 [32, 4], P(('dp', 'expert', 'loop')), may hold values from 0 to 4, as said below
- w_gate: bfloat16 [4, 4096, 768], P('expert', None, 'loop'), may hold values from -0.09375 to 0.09375
- w_up: bfloat16 [4, 4096, 768], P('expert', None, 'loop'), may hold values from -0.09375 to 0.09375
- w_down: bfloat16 [4, 4096, 768], P('expert', None, 'loop'), may hold values from -0.21875 to 0.21875
Outputs:
- grad_rows: bfloat16 [512, 4096], P(('dp', 'expert', 'loop'))
- grad_down: float32 [4, 4096, 768], P('expert', 'dp', 'loop')
Inputs may be any that keep to these rules, and one draw needn't show every extreme that they name: counts[s, e] is how many of the 4 slots of device s for owner e hold rows, filled from slot 0; in each group of 8 consecutive devices one owner, drawn anew, receives 4 rows from every device, and every other owner at most 2 from each device.
All inputs are finite; a program needn't handle non-finite values.
Results may differ from a plain program's by a relative error of at most 0.0095.
Values may be sent and summed in bfloat16 or wider, within the bound.
No kernel may reach another device: no remote copies, remote signals or barrier semaphores. Data moves between devices by JAX's collectives and lax.ppermute only.
A program may use at most 64 MiB of HBM per device.

v0:
```python
import jax
import jax.numpy as jnp
from jax import lax
from jax.sharding import PartitionSpec as P


def local(x_send, cot_send, counts, w_gate, w_up, w_down):
    owner_count = counts.shape[1]
    capacity = x_send.shape[0] // owner_count
    live_slot = (jnp.arange(capacity, dtype=jnp.int32)[None, :] < counts[0][:, None]).reshape(
        owner_count * capacity, 1
    )
    zero_value = jnp.zeros((), jnp.bfloat16)
    inputs = jnp.where(live_slot, x_send, zero_value)
    cotans = jnp.where(live_slot, cot_send, zero_value)
    arrived, arrived_cot = (
        lax.all_to_all(inputs, "expert", split_axis=0, concat_axis=0, tiled=True),
        lax.all_to_all(cotans, "expert", split_axis=0, concat_axis=0, tiled=True),
    )
    gathered, gathered_cot = (
        lax.all_gather(arrived, "loop", axis=0, tiled=True),
        lax.all_gather(arrived_cot, "loop", axis=0, tiled=True),
    )
    gate_local = w_gate[0]
    up_local = w_up[0]
    down_local = w_down[0]
    gate_pre = jnp.dot(gathered, gate_local, preferred_element_type=jnp.float32)
    up_proj = jnp.dot(gathered, up_local, preferred_element_type=jnp.float32)
    sigmoid_gate = jax.nn.sigmoid(gate_pre)
    active = gate_pre * sigmoid_gate
    hidden = (active * up_proj).astype(jnp.bfloat16)
    grad_hidden = jnp.dot(gathered_cot, down_local, preferred_element_type=jnp.float32)
    grad_gate = (
        grad_hidden * up_proj * sigmoid_gate * (1.0 + gate_pre * (1.0 - sigmoid_gate))
    ).astype(jnp.bfloat16)
    grad_upp = (grad_hidden * active).astype(jnp.bfloat16)
    contract_last = (((1,), (1,)), ((), ()))
    contract_first = (((0,), (0,)), ((), ()))
    partial_value = lax.dot_general(
        grad_gate, gate_local, contract_last, preferred_element_type=jnp.float32
    )
    partial_value = partial_value + lax.dot_general(
        grad_upp, up_local, contract_last, preferred_element_type=jnp.float32
    )
    summed = lax.psum_scatter(
        lax.optimization_barrier(partial_value.astype(jnp.bfloat16))
        .astype(jnp.float32)
        .astype(jnp.bfloat16),
        "loop",
        scatter_dimension=0,
        tiled=True,
    )
    grad_rows = lax.all_to_all(summed, "expert", split_axis=0, concat_axis=0, tiled=True)
    column_part = lax.all_to_all(gathered_cot, "dp", split_axis=1, concat_axis=0, tiled=True)
    hidden_all = lax.all_gather(hidden, "dp", axis=0, tiled=True)
    result = lax.dot_general(
        column_part, hidden_all, contract_first, preferred_element_type=jnp.float32
    )
    grad_down = result[None]
    return (grad_rows, grad_down)


def solution(mesh):
    in_specs = (
        P(("dp", "expert", "loop"), None),
        P(("dp", "expert", "loop"), None),
        P(("dp", "expert", "loop"), None),
        P("expert", None, "loop"),
        P("expert", None, "loop"),
        P("expert", None, "loop"),
    )
    out_specs = (P(("dp", "expert", "loop"), None), P("expert", "dp", "loop"))
    return jax.shard_map(local, mesh=mesh, in_specs=in_specs, out_specs=out_specs, check_vma=False)
```

profile of v0, /device:TPU:0, one launch (start us, length us, event | category | flops | bytes accessed | tf_op | source)
XLA Modules:
  0.0 81.4 jit_solution(18439740056307525910)
XLA Ops:
  7.2 0.9 %iota_compare_fusion = pred[4,4]{1,0:T(4,128)(4,1)S(1)} fusion(s32[4]{0:T(128)} %bitcast.33), kind=kLoop, calls=%fused_computation.21 | loop fusion | flops 16 | bytes 32 | tf_op jit(solution)/shard_map/lt | solution.py:10
  8.1 0.1 lt.26
  8.1 1.1 %broadcast_select_fusion.1 = (bf16[16,4096]{1,0:T(8,128)(2,1)S(1)}, bf16[16,4096]{1,0:T(8,128)(2,1)S(1)}) fusion(bf16[16,4096]{1,0:T(8,128)(2,1)} %param.7, pred[16]{0:T(512)(128)(4,1)S(1)} %lt.26, bf16[16,4096]{1,0:T(8,128)(2,1)} %param.6), kind=kLoop, calls=%fused_computation.14 | loop fusion | flops 131072 | bytes 524304 | tf_op jit(solution)/shard_map/jit(_where)/select_n | solution.py:15
  9.2 0.7 all_to_all.38
  9.9 4.3 %all-to-all-start = ((bf16[4,4,4096]{2,1,0:T(4,128)(2,1)}), bf16[4,4,4096]{2,1,0:T(4,128)(2,1)S(1)}, u32[]{:S(2)}, u32[]{:S(2)}) async-start(bf16[4,4,4096]{2,1,0:T(4,128)(2,1)} %all_to_all.38), calls=%async_computation | async-start | bytes 262144 | tf_op jit(solution)/shard_map/all_to_all | solution.py:18
  14.2 0.7 all_to_all.41
  14.9 3.9 %all-to-all-done = bf16[4,4,4096]{2,1,0:T(4,128)(2,1)S(1)} async-done(((bf16[4,4,4096]{2,1,0:T(4,128)(2,1)}), bf16[4,4,4096]{2,1,0:T(4,128)(2,1)S(1)}, u32[]{:S(2)}, u32[]{:S(2)}) %all-to-all-start) | async-done | bytes 131104 | tf_op jit(solution)/shard_map/all_to_all | solution.py:18
  18.8 4.0 %all-to-all-start.1 = ((bf16[4,4,4096]{2,1,0:T(4,128)(2,1)}), bf16[4,4,4096]{2,1,0:T(4,128)(2,1)}, u32[]{:S(2)}, u32[]{:S(2)}) async-start(bf16[4,4,4096]{2,1,0:T(4,128)(2,1)} %all_to_all.41), calls=%async_computation.1 | async-start | bytes 262144 | tf_op jit(solution)/shard_map/all_to_all | solution.py:17
  22.8 6.7 %all_gather.9 = bf16[32,4096]{1,0:T(8,128)(2,1)S(1)} all-gather(bf16[16,4096]{1,0:T(8,128)(2,1)S(1)} %all_to_all.40), channel_id=1, replica_groups=mesh['dp'=4,'expert'=4,'loop'=2] {'loop'}, dimensions={0}, use_global_device_ids=true | all-gather | bytes 393216 | tf_op jit(solution)/shard_map/all_gather | solution.py:22
  29.6 0.9 %all_to_all.43 = bf16[16,4096]{1,0:T(8,128)(2,1)S(1)} reshape(bf16[4,4,4096]{2,1,0:T(4,128)(2,1)} %all-to-all-done.1) | data formatting | bytes 262144 | tf_op jit(solution)/shard_map/all_to_all | solution.py:17
  30.5 6.0 %all_gather.10 = bf16[32,4096]{1,0:T(8,128)(2,1)S(1)} all-gather(bf16[16,4096]{1,0:T(8,128)(2,1)S(1)} %all_to_all.43), channel_id=1, replica_groups=mesh['dp'=4,'expert'=4,'loop'=2] {'loop'}, dimensions={0}, use_global_device_ids=true | all-gather | bytes 393216 | tf_op jit(solution)/shard_map/all_gather | solution.py:21
  36.5 2.4 %fusion.8 = f32[32,384]{1,0:T(8,128)S(1)} fusion(bf16[32,4096]{1,0:T(8,128)(2,1)S(1)} %all_gather.9, bf16[1,4096,384]{2,1,0:T(8,128)(2,1)} %param.11), kind=kOutput, calls=%fused_computation.9 | convolution fusion | flops 100663296 | bytes 3457024 | tf_op jit(solution)/shard_map/dot_general | solution.py:32
  39.0 0.5 fusion.3
  39.5 0.6 multiply_convert_fusion
  40.1 1.1 %fusion.1 = f32[32,4096]{1,0:T(8,128)S(1)} fusion(bf16[1,4096,384]{2,1,0:T(8,128)(2,1)S(1)} %copy-done.1, f32[32,384]{1,0:T(8,128)S(1)} %fusion.3, f32[32,384]{1,0:T(8,128)S(1)} %fusion.8, f32[32,384]{1,0:T(8,128)S(1)} %get-tuple-element.5), kind=kOutput, calls=%fused_computation.2 | convolution fusion | flops 100786176 | bytes 3817472 | tf_op jit(solution)/shard_map/dot_general | solution.py:39
  41.2 1.8 %fusion = bf16[32,4096]{1,0:T(8,128)(2,1)} fusion(f32[32,4096]{1,0:T(8,128)S(1)} %fusion.1, bf16[1,4096,384]{2,1,0:T(8,128)(2,1)S(1)} %copy-done, f32[32,384]{1,0:T(8,128)S(1)} %fusion.8, f32[32,384]{1,0:T(8,128)S(1)} %fusion.3), kind=kOutput, calls=%fused_computation.1 | convolution fusion | flops 100999168 | bytes 4030464 | tf_op jit(solution)/shard_map/dot_general | solution.py:42
  43.0 0.7 copy.12
  43.7 4.9 %all-to-all-start.3 = ((bf16[32,4,1024]{2,0,1:T(8,128)(2,1)}), bf16[32,4,1024]{2,0,1:T(8,128)(2,1)S(1)}, u32[]{:S(2)}, u32[]{:S(2)}) async-start(bf16[32,4,1024]{2,0,1:T(8,128)(2,1)} %bitcast.31), calls=%async_computation.4 | async-start | bytes 524288 | tf_op jit(solution)/shard_map/all_to_all | solution.py:54
  48.6 15.7 %all_gather.11 = bf16[128,384]{1,0:T(8,128)(2,1)} all-gather(bf16[32,384]{1,0:T(8,128)(2,1)S(1)} %get-tuple-element.4), channel_id=1, replica_groups=mesh['dp'=4,'expert'=4,'loop'=2] {'dp'}, dimensions={0}, use_global_device_ids=true | all-gather | bytes 122880 | tf_op jit(solution)/shard_map/all_gather | solution.py:55
  64.3 1.6 %all_to_all.44 = bf16[4,4,4096]{2,1,0:T(4,128)(2,1)} reshape(bf16[16,4096]{1,0:T(8,128)(2,1)} %reduce-scatter.2.cloned.1.call-done) | data formatting | bytes 262144 | tf_op jit(solution)/shard_map/all_to_all | solution.py:53
  66.0 3.3 %all-to-all-start.2 = ((bf16[4,4,4096]{2,1,0:T(4,128)(2,1)}), bf16[4,4,4096]{2,1,0:T(4,128)(2,1)S(1)}, u32[]{:S(2)}, u32[]{:S(2)}) async-start(bf16[4,4,4096]{2,1,0:T(4,128)(2,1)} %all_to_all.44), calls=%async_computation.3 | async-start | bytes 262144 | tf_op jit(solution)/shard_map/all_to_all | solution.py:53
  69.3 2.4 %convolution_bitcast_fusion = f32[1,1024,384]{2,1,0:T(8,128)} fusion(bf16[128,1024]{1,0:T(8,128)(2,1)S(1)} %bitcast.32, bf16[128,384]{1,0:T(8,128)(2,1)} %all_gather.11), kind=kOutput, calls=%fused_computation.11 | convolution fusion | flops 100663296 | bytes 1933312 | tf_op jit(solution)/shard_map/dot_general | solution.py:56
  71.7 2.1 %all-to-all-done.2 = bf16[4,4,4096]{2,1,0:T(4,128)(2,1)S(1)} async-done(((bf16[4,4,4096]{2,1,0:T(4,128)(2,1)}), bf16[4,4,4096]{2,1,0:T(4,128)(2,1)S(1)}, u32[]{:S(2)}, u32[]{:S(2)}) %all-to-all-start.2) | async-done | bytes 131104 | tf_op jit(solution)/shard_map/all_to_all | solution.py:53
  73.9 0.7 all_to_all.46
  (10 shorter events, 0.1 us)
Async XLA Ops:
  7.2 32.4 %copy-start = (bf16[1,4096,384]{2,1,0:T(8,128)(2,1)S(1)}, bf16[1,4096,384]{2,1,0:T(8,128)(2,1)}, u32[]{:S(2)}) copy-start(bf16[1,4096,384]{2,1,0:T(8,128)(2,1)} %param.10) | copy-start | bytes 9437188
  9.9 8.9 %all-to-all-start = ((bf16[4,4,4096]{2,1,0:T(4,128)(2,1)}), bf16[4,4,4096]{2,1,0:T(4,128)(2,1)S(1)}, u32[]{:S(2)}, u32[]{:S(2)}) async-start(bf16[4,4,4096]{2,1,0:T(4,128)(2,1)} %all_to_all.38), calls=%async_computation | async-start | bytes 262144 | tf_op jit(solution)/shard_map/all_to_all | solution.py:18
  18.8 10.8 %all-to-all-start.1 = ((bf16[4,4,4096]{2,1,0:T(4,128)(2,1)}), bf16[4,4,4096]{2,1,0:T(4,128)(2,1)}, u32[]{:S(2)}, u32[]{:S(2)}) async-start(bf16[4,4,4096]{2,1,0:T(4,128)(2,1)} %all_to_all.41), calls=%async_computation.1 | async-start | bytes 262144 | tf_op jit(solution)/shard_map/all_to_all | solution.py:17
  22.7 41.6 %reduce-scatter.2.cloned.1.call-start = ((), (), s32[]{:S(2)}) async-start(), calls=%async_computation.5 | async-start | bytes 393216 | tf_op jit(solution)/shard_map/reduce_scatter | solution.py:45
  30.5 8.4 %copy-start.1 = (bf16[1,4096,384]{2,1,0:T(8,128)(2,1)S(1)}, bf16[1,4096,384]{2,1,0:T(8,128)(2,1)}, u32[]{:S(2)}) copy-start(bf16[1,4096,384]{2,1,0:T(8,128)(2,1)} %param.9) | copy-start | bytes 9437188
  43.7 22.3 %all-to-all-start.3 = ((bf16[32,4,1024]{2,0,1:T(8,128)(2,1)}), bf16[32,4,1024]{2,0,1:T(8,128)(2,1)S(1)}, u32[]{:S(2)}, u32[]{:S(2)}) async-start(bf16[32,4,1024]{2,0,1:T(8,128)(2,1)} %bitcast.31), calls=%async_computation.4 | async-start | bytes 524288 | tf_op jit(solution)/shard_map/all_to_all | solution.py:54
  66.0 7.9 %all-to-all-start.2 = ((bf16[4,4,4096]{2,1,0:T(4,128)(2,1)}), bf16[4,4,4096]{2,1,0:T(4,128)(2,1)S(1)}, u32[]{:S(2)}, u32[]{:S(2)}) async-start(bf16[4,4,4096]{2,1,0:T(4,128)(2,1)} %all_to_all.44), calls=%async_computation.3 | async-start | bytes 262144 | tf_op jit(solution)/shard_map/all_to_all | solution.py:53
Sparse Core Ops, SparseCore 0:
  43.1 13.1 reduce-scatter.1
where the time goes:
time: 82 us; the launch traced here: 81.4 us
  blocking collectives  28.5 us (35%)
  starting transfers between devices  16.5 us (20%)
  between operations  14.1 us (17%)
  matrix products  8.8 us (11%)
  waiting for transfers between devices  6.05 us (7%)
  local copies, waits for them, and re-layouts  5.53 us (7%)
  other arithmetic  1.94 us (2%)
    all_gather x1, blocking collectives, local(): hidden_all = lax.all_gather(hidden, 'dp', axis=0, tiled=True)  15.7 us
    all_gather x1, blocking collectives, local(): lax.all_gather(arrived_cot, 'loop', axis=0, tiled=True)  6.73 us
    all_gather x1, blocking collectives, local(): lax.all_gather(arrived, 'loop', axis=0, tiled=True)  6 us
    all_to_all x1, starting transfers between devices, local(): lax.all_to_all(gathered_cot, 'dp', split_axis=1, concat_axis=0, tiled=True)  4.9 us
    all_to_all x1, starting transfers between devices, local(): lax.all_to_all(cotans, 'expert', split_axis=0, concat_axis=0, tiled=True)  4.26 us
    all_to_all x1, starting transfers between devices, local(): lax.all_to_all(inputs, 'expert', split_axis=0, concat_axis=0, tiled=True)  3.95 us
    all_to_all x1, waiting for transfers between devices, local(): lax.all_to_all(cotans, 'expert', split_axis=0, concat_axis=0, tiled=True)  3.89 us
    all_to_all x1, starting transfers between devices, local(): lax.all_to_all(summed, 'expert', split_axis=0, concat_axis=0, tiled=True)  3.33 us
  transfers between devices with their start and end apart: 5, of which 2 were waited for; matrix products, arithmetic and copies ran while one was open for 4% of the time, Pallas kernels for 0%

commit v1 on v0

--- a/solution.py
+++ b/solution.py
@@ -2,6 +2,28 @@
 import jax.numpy as jnp
 from jax import lax
 from jax.sharding import PartitionSpec as P
+
+
+def split_up(x, dim, size):
+    before, after = (x.shape[:dim], x.shape[dim + 1 :])
+    return jnp.moveaxis(x.reshape(*before, size, -1, *after), dim, 0)
+
+
+def laid_out(tiles, dim):
+    tiles = jnp.moveaxis(tiles, 0, dim)
+    shape = tiles.shape
+    return tiles.reshape(*shape[:dim], shape[dim] * shape[dim + 1], *shape[dim + 2 :])
+
+
+def sent_to_each(value, axis, split_dim, concat_dim):
+    size, index = (lax.axis_size(axis), lax.axis_index(axis))
+    blocks = split_up(value, split_dim, size)
+    finished = [blocks[index]]
+    for step in range(1, size):
+        sent = blocks[(index + step) % size]
+        finished.append(lax.ppermute(sent, axis, [(i, (i + step) % size) for i in range(size)]))
+    blocks = jnp.stack(finished)[(index - jnp.arange(size)) % size]
+    return laid_out(blocks, concat_dim)
 
 
 def local(x_send, cot_send, counts, w_gate, w_up, w_down):
@@ -15,7 +37,7 @@
     cotans = jnp.where(live_slot, cot_send, zero_value)
     arrived, arrived_cot = (
         lax.all_to_all(inputs, "expert", split_axis=0, concat_axis=0, tiled=True),
-        lax.all_to_all(cotans, "expert", split_axis=0, concat_axis=0, tiled=True),
+        sent_to_each(cotans, "expert", 0, 0),
     )
     gathered, gathered_cot = (
         lax.all_gather(arrived, "loop", axis=0, tiled=True),

time: 82 us -> 80.7 us (0.984)
  waiting for transfers between devices: 6.05 us -> 2.17 us
  matrix products: 8.8 us -> 11.5 us
  starting transfers between devices: 16.5 us -> 15.5 us
    all_to_all x1 -> x0, starting transfers between devices: 4.26 us -> none  [local(): lax.all_to_all(cotans, 'expert', split_axis=0, concat_axis=0, tiled=True)]
    all_to_all x1 -> x0, waiting for transfers between devices: 3.89 us -> none  [local(): lax.all_to_all(cotans, 'expert', split_axis=0, concat_axis=0, tiled=True)]
    ppermute x0 -> x3, starting transfers between devices: none -> 3.28 us  [sent_to_each(): lax.ppermute(sent, axis, [(i, (i + step) % size) for i in range(size)])]
    dot_general x1, matrix products: 0.55 us -> 2.58 us  [local(): gate_pre = jnp.dot(gathered, gate_local, preferred_element_type=jnp.float32)]
  transfers between devices with their start and end apart: 5 -> 7, of which waited for: 2 -> 1; matrix products, arithmetic and copies ran while one was open for 4% -> 9% of each run, Pallas kernels for 0% -> 0%
where the time goes in v1:
time: 80.7 us; the launch traced here: 80.2 us
  blocking collectives  29.2 us (36%)
  starting transfers between devices  15.5 us (19%)
  between operations  14.2 us (18%)
  matrix products  11.5 us (14%)
  local copies, waits for them, and re-layouts  5.6 us (7%)
  waiting for transfers between devices  2.17 us (3%)
  other arithmetic  2.07 us (3%)
    all_gather x1, blocking collectives, local(): hidden_all = lax.all_gather(hidden, 'dp', axis=0, tiled=True)  16.3 us
    all_gather x1, blocking collectives, local(): lax.all_gather(arrived_cot, 'loop', axis=0, tiled=True)  6.67 us
    all_gather x1, blocking collectives, local(): lax.all_gather(arrived, 'loop', axis=0, tiled=True)  6.26 us
    all_to_all x1, starting transfers between devices, local(): lax.all_to_all(gathered_cot, 'dp', split_axis=1, concat_axis=0, tiled=True)  4.87 us
    all_to_all x1, starting transfers between devices, local(): lax.all_to_all(inputs, 'expert', split_axis=0, concat_axis=0, tiled=True)  3.94 us
    all_to_all x1, starting transfers between devices, local(): lax.all_to_all(summed, 'expert', split_axis=0, concat_axis=0, tiled=True)  3.33 us
    ppermute x3, starting transfers between devices, sent_to_each(): lax.ppermute(sent, axis, [(i, (i + step) % size) for i in range(size)])  3.28 us
    dot_general x1, matrix products, local(): jnp.dot(gathered_cot, down_local, preferred_element_type=jnp.float32)  3.06 us
  transfers between devices with their start and end apart: 7, of which 1 were waited for; matrix products, arithmetic and copies ran while one was open for 9% of the time, Pallas kernels for 0%

profile of v1, /device:TPU:0, one launch (start us, length us, event | category | flops | bytes accessed | tf_op | source)
XLA Modules:
  0.0 80.2 jit_solution(14535884734257212106)
XLA Ops:
  7.2 0.9 %iota_compare_fusion = pred[4,4]{1,0:T(4,128)(4,1)S(1)} fusion(s32[4]{0:T(128)} %bitcast.47), kind=kLoop, calls=%fused_computation.30 | loop fusion | flops 16 | bytes 32 | tf_op jit(solution)/shard_map/lt | solution.py:32
  8.2 1.1 %broadcast_select_fusion.1 = (bf16[16,4096]{1,0:T(8,128)(2,1)S(1)}, bf16[16,4096]{1,0:T(8,128)(2,1)S(1)}) fusion(bf16[16,4096]{1,0:T(8,128)(2,1)} %param.7, pred[16]{0:T(512)(128)(4,1)S(1)} %lt.68, bf16[16,4096]{1,0:T(8,128)(2,1)} %param.6), kind=kLoop, calls=%fused_computation.16 | loop fusion | flops 131072 | bytes 524304 | tf_op jit(solution)/shard_map/jit(_where)/select_n | solution.py:37
  9.4 2.5 %collective-permute-start.2 = (bf16[4,4096]{1,0:T(4,128)(2,1)S(1)}, bf16[4,4096]{1,0:T(4,128)(2,1)S(1)}, u32[]{:S(2)}, u32[]{:S(2)}) collective-permute-start(bf16[4,4096]{1,0:T(4,128)(2,1)S(1)} %get-tuple-element.3), channel_id=1, source_target_pairs={{0,6},{2,0},{4,2},{6,4},{1,7},{3,1},{5,3},{7,5},{8,14},{10,8},{12,... | collective-permute-start | bytes 98312 | tf_op jit(solution)/shard_map/ppermute | solution.py:24
  11.9 0.6 collective-permute-start.1
  12.5 0.2 collective-permute-start
  12.7 0.7 all_to_all.30
  13.4 3.9 %all-to-all-start = ((bf16[4,4,4096]{2,1,0:T(4,128)(2,1)}), bf16[4,4,4096]{2,1,0:T(4,128)(2,1)}, u32[]{:S(2)}, u32[]{:S(2)}) async-start(bf16[4,4,4096]{2,1,0:T(4,128)(2,1)} %all_to_all.30), calls=%async_computation | async-start | bytes 262144 | tf_op jit(solution)/shard_map/all_to_all | solution.py:39
  17.6 0.7 gather_fusion
  18.3 6.7 %all_gather.9 = bf16[32,4096]{1,0:T(8,128)(2,1)S(1)} all-gather(bf16[16,4096]{1,0:T(8,128)(2,1)S(1)} %reshape.83), channel_id=1, replica_groups=mesh['dp'=4,'expert'=4,'loop'=2] {'loop'}, dimensions={0}, use_global_device_ids=true | all-gather | bytes 393216 | tf_op jit(solution)/shard_map/all_gather | solution.py:44
  24.9 3.1 %fusion.8 = f32[32,384]{1,0:T(8,128)} fusion(bf16[32,4096]{1,0:T(8,128)(2,1)S(1)} %all_gather.9, bf16[1,4096,384]{2,1,0:T(8,128)(2,1)} %param.11), kind=kOutput, calls=%fused_computation.10 | convolution fusion | flops 100663296 | bytes 3457024 | tf_op jit(solution)/shard_map/dot_general | solution.py:54
  28.0 0.9 %all_to_all.32 = bf16[16,4096]{1,0:T(8,128)(2,1)S(1)} reshape(bf16[4,4,4096]{2,1,0:T(4,128)(2,1)} %all-to-all-done) | data formatting | bytes 262144 | tf_op jit(solution)/shard_map/all_to_all | solution.py:39
  28.9 6.3 %all_gather.10 = bf16[32,4096]{1,0:T(8,128)(2,1)S(1)} all-gather(bf16[16,4096]{1,0:T(8,128)(2,1)S(1)} %all_to_all.32), channel_id=1, replica_groups=mesh['dp'=4,'expert'=4,'loop'=2] {'loop'}, dimensions={0}, use_global_device_ids=true | all-gather | bytes 393216 | tf_op jit(solution)/shard_map/all_gather | solution.py:43
  35.2 2.6 %fusion.3 = f32[32,384]{1,0:T(8,128)S(1)} fusion(bf16[32,4096]{1,0:T(8,128)(2,1)S(1)} %all_gather.10, bf16[1,4096,384]{2,1,0:T(8,128)(2,1)} %param.9), kind=kOutput, calls=%fused_computation.5 | convolution fusion | flops 100663296 | bytes 3457024 | tf_op jit(solution)/shard_map/dot_general | solution.py:49
  37.8 0.6 multiply_convert_fusion
  38.4 1.1 %fusion.1 = f32[32,4096]{1,0:T(8,128)S(1)} fusion(bf16[1,4096,384]{2,1,0:T(8,128)(2,1)S(1)} %copy-done.1, f32[32,384]{1,0:T(8,128)S(1)} %fusion.3, f32[32,384]{1,0:T(8,128)S(1)} %copy-done.2, f32[32,384]{1,0:T(8,128)S(1)} %get-tuple-element.9), kind=kOutput, calls=%fused_computation.3 | convolution fusion | flops 100786176 | bytes 3817472 | tf_op jit(solution)/shard_map/dot_general | solution.py:61
  39.4 1.8 %fusion = bf16[32,4096]{1,0:T(8,128)(2,1)} fusion(f32[32,4096]{1,0:T(8,128)S(1)} %fusion.1, bf16[1,4096,384]{2,1,0:T(8,128)(2,1)S(1)} %copy-done, f32[32,384]{1,0:T(8,128)S(1)} %copy-done.2, f32[32,384]{1,0:T(8,128)S(1)} %fusion.3), kind=kOutput, calls=%fused_computation.2 | convolution fusion | flops 100999168 | bytes 4030464 | tf_op jit(solution)/shard_map/dot_general | solution.py:64
  41.3 0.7 copy.12
  42.0 4.9 %all-to-all-start.2 = ((bf16[32,4,1024]{2,0,1:T(8,128)(2,1)}), bf16[32,4,1024]{2,0,1:T(8,128)(2,1)S(1)}, u32[]{:S(2)}, u32[]{:S(2)}) async-start(bf16[32,4,1024]{2,0,1:T(8,128)(2,1)} %bitcast.42), calls=%async_computation.3 | async-start | bytes 524288 | tf_op jit(solution)/shard_map/all_to_all | solution.py:76
  46.8 16.3 %all_gather.11 = bf16[128,384]{1,0:T(8,128)(2,1)} all-gather(bf16[32,384]{1,0:T(8,128)(2,1)S(1)} %get-tuple-element.8), channel_id=1, replica_groups=mesh['dp'=4,'expert'=4,'loop'=2] {'dp'}, dimensions={0}, use_global_device_ids=true | all-gather | bytes 122880 | tf_op jit(solution)/shard_map/all_gather | solution.py:77
  63.1 1.6 %all_to_all.33 = bf16[4,4,4096]{2,1,0:T(4,128)(2,1)} reshape(bf16[16,4096]{1,0:T(8,128)(2,1)} %reduce-scatter.2.cloned.1.call-done) | data formatting | bytes 262144 | tf_op jit(solution)/shard_map/all_to_all | solution.py:75
  64.8 3.3 %all-to-all-start.1 = ((bf16[4,4,4096]{2,1,0:T(4,128)(2,1)}), bf16[4,4,4096]{2,1,0:T(4,128)(2,1)S(1)}, u32[]{:S(2)}, u32[]{:S(2)}) async-start(bf16[4,4,4096]{2,1,0:T(4,128)(2,1)} %all_to_all.33), calls=%async_computation.2 | async-start | bytes 262144 | tf_op jit(solution)/shard_map/all_to_all | solution.py:75
  68.1 2.4 %convolution_bitcast_fusion = f32[1,1024,384]{2,1,0:T(8,128)} fusion(bf16[128,1024]{1,0:T(8,128)(2,1)S(1)} %bitcast.43, bf16[128,384]{1,0:T(8,128)(2,1)} %all_gather.11), kind=kOutput, calls=%fused_computation.12 | convolution fusion | flops 100663296 | bytes 1933312 | tf_op jit(solution)/shard_map/dot_general | solution.py:78
  70.5 2.1 %all-to-all-done.1 = bf16[4,4,4096]{2,1,0:T(4,128)(2,1)S(1)} async-done(((bf16[4,4,4096]{2,1,0:T(4,128)(2,1)}), bf16[4,4,4096]{2,1,0:T(4,128)(2,1)S(1)}, u32[]{:S(2)}, u32[]{:S(2)}) %all-to-all-start.1) | async-done | bytes 131104 | tf_op jit(solution)/shard_map/all_to_all | solution.py:75
  72.7 0.7 all_to_all.35
  (21 shorter events, 0.5 us)
Async XLA Ops:
  7.2 30.6 %copy-start = (bf16[1,4096,384]{2,1,0:T(8,128)(2,1)S(1)}, bf16[1,4096,384]{2,1,0:T(8,128)(2,1)}, u32[]{:S(2)}) copy-start(bf16[1,4096,384]{2,1,0:T(8,128)(2,1)} %param.10) | copy-start | bytes 9437188
  9.4 8.0 %collective-permute-start.2 = (bf16[4,4096]{1,0:T(4,128)(2,1)S(1)}, bf16[4,4096]{1,0:T(4,128)(2,1)S(1)}, u32[]{:S(2)}, u32[]{:S(2)}) collective-permute-start(bf16[4,4096]{1,0:T(4,128)(2,1)S(1)} %get-tuple-element.3), channel_id=1, source_target_pairs={{0,6},{2,0},{4,2},{6,4},{1,7},{3,1},{5,3},{7,5},{8,14},{10,8},{12,... | collective-permute-start | bytes 98312 | tf_op jit(solution)/shard_map/ppermute | solution.py:24
  11.9 5.5 %collective-permute-start.1 = (bf16[4,4096]{1,0:T(4,128)(2,1)S(1)}, bf16[4,4096]{1,0:T(4,128)(2,1)S(1)}, u32[]{:S(2)}, u32[]{:S(2)}) collective-permute-start(bf16[4,4096]{1,0:T(4,128)(2,1)S(1)} %get-tuple-element.4), channel_id=1, source_target_pairs={{0,4},{2,6},{4,0},{6,2},{1,5},{3,7},{5,1},{7,3},{8,12},{10,14},{12... | collective-permute-start | bytes 98312 | tf_op jit(solution)/shard_map/ppermute | solution.py:24
  12.5 4.9 %collective-permute-start = (bf16[4,4096]{1,0:T(4,128)(2,1)S(1)}, bf16[4,4096]{1,0:T(4,128)(2,1)S(1)}, u32[]{:S(2)}, u32[]{:S(2)}) collective-permute-start(bf16[4,4096]{1,0:T(4,128)(2,1)S(1)} %get-tuple-element.5), channel_id=1, source_target_pairs={{0,2},{2,4},{4,6},{6,0},{1,3},{3,5},{5,7},{7,1},{8,10},{10,12},{12... | collective-permute-start | bytes 98312 | tf_op jit(solution)/shard_map/ppermute | solution.py:24
  13.4 14.6 %all-to-all-start = ((bf16[4,4,4096]{2,1,0:T(4,128)(2,1)}), bf16[4,4,4096]{2,1,0:T(4,128)(2,1)}, u32[]{:S(2)}, u32[]{:S(2)}) async-start(bf16[4,4,4096]{2,1,0:T(4,128)(2,1)} %all_to_all.30), calls=%async_computation | async-start | bytes 262144 | tf_op jit(solution)/shard_map/all_to_all | solution.py:39
  17.3 45.8 %reduce-scatter.2.cloned.1.call-start = ((), (), s32[]{:S(2)}) async-start(), calls=%async_computation.4 | async-start | bytes 393216 | tf_op jit(solution)/shard_map/reduce_scatter | solution.py:67
  35.2 3.2 %copy-start.1 = (bf16[1,4096,384]{2,1,0:T(8,128)(2,1)S(1)}, bf16[1,4096,384]{2,1,0:T(8,128)(2,1)}, u32[]{:S(2)}) copy-start(bf16[1,4096,384]{2,1,0:T(8,128)(2,1)} %param.9) | copy-start | bytes 9437188
  35.2 3.2 %copy-start.2 = (f32[32,384]{1,0:T(8,128)S(1)}, f32[32,384]{1,0:T(8,128)}, u32[]{:S(2)}) copy-start(f32[32,384]{1,0:T(8,128)} %fusion.8) | copy-start | bytes 147460
  42.0 22.8 %all-to-all-start.2 = ((bf16[32,4,1024]{2,0,1:T(8,128)(2,1)}), bf16[32,4,1024]{2,0,1:T(8,128)(2,1)S(1)}, u32[]{:S(2)}, u32[]{:S(2)}) async-start(bf16[32,4,1024]{2,0,1:T(8,128)(2,1)} %bitcast.42), calls=%async_computation.3 | async-start | bytes 524288 | tf_op jit(solution)/shard_map/all_to_all | solution.py:76
  64.8 7.9 %all-to-all-start.1 = ((bf16[4,4,4096]{2,1,0:T(4,128)(2,1)}), bf16[4,4,4096]{2,1,0:T(4,128)(2,1)S(1)}, u32[]{:S(2)}, u32[]{:S(2)}) async-start(bf16[4,4,4096]{2,1,0:T(4,128)(2,1)} %all_to_all.33), calls=%async_computation.2 | async-start | bytes 262144 | tf_op jit(solution)/shard_map/all_to_all | solution.py:75
Sparse Core Ops, SparseCore 0:
  41.4 12.2 reduce-scatter.1
